TPU v7x, 256 devices: a whole 4x4x8 slice. The times are simulated.
256 devices in a mesh: row: 16 (over y, x), col: 2 (over core), ctx: 8 (over z).
Axes of the slice: x: 4, y: 4, z: 8, core: 2. Of those that a mesh axis runs over, the one named last changes fastest.
Arguments:
- queries: bfloat16 [8192, 6144], P(('col', 'ctx'), 'row'), may hold values from -16 to 16
- keys: bfloat16 [8192, 6144], P(('col', 'ctx'), 'row'), may hold values from -16 to 16
- values: bfloat16 [8192, 6144], P(('col', 'ctx'), 'row'), may hold values from -6 to 6
- out_weight: bfloat16 [6144, 6144], P('col', 'row'), may hold values from -0.078125 to 0.078125
- cotangent: bfloat16 [8192, 6144], P(('col', 'ctx'), 'row'), may hold values from -0.125 to 0.125
- block_mask: int32 [16, 16], replicated, may hold values from 0 to 1, as said below
Outputs:
- mixed_out: bfloat16 [8192, 6144], P(('col', 'ctx'), 'row')
- grad_weight: bfloat16 [6144, 6144], P(('col', 'ctx'), 'row')
Inputs may be any that keep to these rules, and one draw needn't show every extreme that they name: block_mask[i, i] is 1 for every block i, and block_mask[i, j] is 0 for j > i.
All inputs are finite; a program needn't handle non-finite values.
Results may differ from a plain program's by a relative error of at most 0.013.
Values may be sent and summed in bfloat16 or wider, within the bound.
A program may use at most 64 MiB of HBM per device.

v0:
```python
import math
import jax
import jax.numpy as jnp
from jax import lax
from jax.sharding import PartitionSpec as P

HD = 128
BLOCK = 512
NEGATIVE_FILL = -1e30


def attend_block(carried, query_heads, key_block, value_block, allowed, score_scale):
    run_max, run_sum, weighted = carried
    tok_rows, head_count, head_size = query_heads.shape
    key_heads = key_block.reshape(key_block.shape[0], head_count, head_size)
    value_heads = value_block.reshape(value_block.shape[0], head_count, head_size)
    scores = (
        jnp.einsum("thd,uhd->thu", query_heads, key_heads, preferred_element_type=jnp.float32)
        * score_scale
    )
    scores = jnp.where(allowed[:, None, None], scores, NEGATIVE_FILL)
    new_max = jnp.maximum(run_max, jnp.max(scores, axis=2))
    correction = jnp.exp(run_max - new_max)
    weights = jnp.where(allowed[:, None, None], jnp.exp(scores - new_max[:, :, None]), 0.0)
    new_sum = run_sum * correction + jnp.sum(weights, axis=2)
    product = jnp.einsum(
        "thu,uhd->thd",
        weights.astype(jnp.bfloat16),
        value_heads,
        preferred_element_type=jnp.float32,
    )
    new_weighted = weighted * correction[:, :, None] + product
    return (new_max, new_sum, new_weighted)


def body(queries, keys, values, out_weight, cotangent, block_mask):
    tok_rows, feature_width = queries.shape
    head_count = feature_width // HD
    query_heads = queries.reshape(tok_rows, head_count, HD)
    score_scale = 1.0 / math.sqrt(HD)
    local_blocks = tok_rows // BLOCK
    first_block = lax.axis_index(("col", "ctx")) * local_blocks
    local_mask = lax.dynamic_slice_in_dim(block_mask, first_block, local_blocks, 0)
    start_state = (
        jnp.full((tok_rows, head_count), NEGATIVE_FILL, jnp.float32),
        jnp.zeros((tok_rows, head_count), jnp.float32),
        jnp.zeros((tok_rows, head_count, HD), jnp.float32),
    )
    key_piece = lax.all_gather(keys, ("col", "ctx"), axis=0, tiled=True)
    value_piece = lax.all_gather(values, ("col", "ctx"), axis=0, tiled=True)
    block_count = key_piece.shape[0] // BLOCK
    key_stack = key_piece.reshape(block_count, BLOCK, feature_width)
    value_stack = value_piece.reshape(block_count, BLOCK, feature_width)
    block_columns = jnp.arange(block_count, dtype=jnp.int32)

    def one_block(state_in, entries):
        key_block, value_block, block_column = entries
        mask_column = lax.dynamic_index_in_dim(local_mask, block_column, 1, keepdims=False)
        allowed = jnp.repeat(mask_column, BLOCK, total_repeat_length=tok_rows) == 1
        updated = attend_block(state_in, query_heads, key_block, value_block, allowed, score_scale)
        return (updated, None)

    state_out, _ = lax.scan(one_block, start_state, (key_stack, value_stack, block_columns))
    run_max, run_sum, weighted = state_out
    attended = (
        (weighted / run_sum[:, :, None]).reshape(tok_rows, feature_width).astype(jnp.bfloat16)
    )
    all_heads = lax.all_gather(attended, "row", axis=1, tiled=True)
    head_columns = all_heads
    mixed_out = jnp.dot(
        head_columns,
        lax.all_gather(out_weight, "col", axis=0, tiled=True),
        preferred_element_type=jnp.float32,
    )
    head_columns = all_heads
    grad_weight = lax.psum_scatter(
        lax.dot_general(
            head_columns, cotangent, (((0,), (0,)), ((), ())), preferred_element_type=jnp.float32
        ),
        ("col", "ctx"),
        scatter_dimension=0,
        tiled=True,
    )
    return (mixed_out.astype(jnp.bfloat16), grad_weight.astype(jnp.bfloat16))


def solution(mesh):
    in_specs = (
        P(("col", "ctx"), "row"),
        P(("col", "ctx"), "row"),
        P(("col", "ctx"), "row"),
        P("col", "row"),
        P(("col", "ctx"), "row"),
        P(),
    )
    out_specs = (P(("col", "ctx"), "row"), P(("col", "ctx"), "row"))
    return jax.shard_map(body, mesh=mesh, in_specs=in_specs, out_specs=out_specs, check_vma=False)
```

profile of v0, /device:TPU:1, one launch (start us, length us, event | category | flops | bytes accessed | tf_op | source)
XLA Modules:
  0.0 622.6 jit_solution(9049366893125646251)
XLA Ops:
  12.0 48.1 %all-gather.5.cloned.1.call-done = bf16[8192,384]{1,0:T(8,128)(2,1)} async-done(((bf16[512,384]{1,0:T(8,128)(2,1)}), bf16[8192,384]{1,0:T(8,128)(2,1)}) %all-gather.5.cloned.1.call-update) | async-done | bytes 6291472 | tf_op jit(solution)/shard_map/all_gather | solution.py:49
  60.1 46.5 %all-gather.7.cloned.1.call-done = bf16[8192,384]{1,0:T(8,128)(2,1)} async-done(((bf16[512,384]{1,0:T(8,128)(2,1)}), bf16[8192,384]{1,0:T(8,128)(2,1)}) %all-gather.7.cloned.1.call-update) | async-done | bytes 6291472 | tf_op jit(solution)/shard_map/all_gather | solution.py:50
  107.2 304.6 %while.22 = (s32[]{:T(128)}, f32[512,3]{0,1:T(4,128)}, f32[512,3]{0,1:T(4,128)}, f32[512,3,128]{0,2,1:T(8,128)}, s32[16]{0:T(128)}, /*index=5*/s32[1,16]{1,0:T(1...) while((s32[]{:T(128)}, f32[512,3]{0,1:T(4,128)}, ...), condition=%wide.region_3.4_spmd.clone, body=%wide.region_0.3_spmd.clone.sunk | while | flops 413474304 | bytes 15433919 | solution.py:63
  120.7 3.4 fusion.42
  139.5 3.7 fusion.42
  158.7 3.7 fusion.42
  177.8 3.7 fusion.42
  197.0 3.7 fusion.42
  216.1 3.7 fusion.42
  235.2 3.7 fusion.42
  254.4 3.7 fusion.42
  273.5 3.7 fusion.42
  292.7 3.7 fusion.42
  311.8 3.7 fusion.42
  330.9 3.7 fusion.42
  350.1 3.7 fusion.42
  369.2 3.7 fusion.42
  388.3 3.7 fusion.42
  407.5 3.7 fusion.42
  414.4 64.1 %all-gather.9.cloned.1.call-done = bf16[512,6144]{0,1:T(8,128)(2,1)} async-done(((bf16[512,384]{0,1:T(8,128)(2,1)}), bf16[512,6144]{0,1:T(8,128)(2,1)}) %all-gather.9.cloned.1.call-update) | async-done | bytes 6291472 | tf_op jit(solution)/shard_map/all_gather | solution.py:68
  478.5 9.9 %fusion.19 = f32[6144,384]{1,0:T(8,128)} fusion(bf16[512,6144]{0,1:T(8,128)(2,1)} %all-gather.9.cloned.1.call-done, bf16[512,384]{1,0:T(8,128)(2,1)S(1)} %copy-done), kind=kOutput, calls=%fused_computation.27 | convolution fusion | flops 2415919104 | bytes 16121856 | tf_op jit(solution)/shard_map/dot_general | solution.py:77
  488.4 12.0 %all-gather.11.cloned.1.call-done = bf16[6144,384]{1,0:T(8,128)(2,1)} async-done(((bf16[3072,384]{1,0:T(8,128)(2,1)}), bf16[6144,384]{1,0:T(8,128)(2,1)}) %all-gather.11.cloned.1.call-update) | async-done | bytes 4718608 | tf_op jit(solution)/shard_map/all_gather | solution.py:72
  500.4 8.3 %convolution_convert_fusion = bf16[512,384]{1,0:T(8,128)(2,1)} fusion(bf16[512,6144]{0,1:T(8,128)(2,1)} %all-gather.9.cloned.1.call-done, bf16[6144,384]{1,0:T(8,128)(2,1)} %all-gather.11.cloned.1.call-done), kind=kOutput, calls=%fused_computation.23 | convolution fusion | flops 2416115712 | bytes 11403264 | tf_op jit(solution)/shard_map/dot_general | solution.py:70
  508.7 105.5 %reduce-scatter.2.cloned.1.call-done = f32[384,384]{1,0:T(8,128)} async-done(((f32[6144,384]{1,0:T(8,128)}), f32[384,384]{1,0:T(8,128)}) %reduce-scatter.2.cloned.1.call-update) | async-done | bytes 589840 | tf_op jit(solution)/shard_map/reduce_scatter | solution.py:76
  (181 shorter events, 226.0 us)
Async XLA Ops:
  7.2 471.3 %copy-start = (bf16[512,384]{1,0:T(8,128)(2,1)S(1)}, bf16[512,384]{1,0:T(8,128)(2,1)}, u32[]{:S(2)}) copy-start(bf16[512,384]{1,0:T(8,128)(2,1)} %param.16) | copy-start | bytes 1179652
  7.2 53.0 %all-gather.5.cloned.1.call-start = ((), (), s32[]{:S(2)}) async-start(), calls=%async_computation.1 | async-start | bytes 6684672 | tf_op jit(solution)/shard_map/all_gather | solution.py:49
  7.9 98.7 %all-gather.7.cloned.1.call-start = ((), (), s32[]{:S(2)}) async-start(), calls=%async_computation.2 | async-start | bytes 6684672 | tf_op jit(solution)/shard_map/all_gather | solution.py:50
  8.7 469.8 %all-gather.9.cloned.1.call-start = ((), (), s32[]{:S(2)}) async-start(), calls=%async_computation.3 | async-start | bytes 6684672 | tf_op jit(solution)/shard_map/all_gather | solution.py:68
  413.7 86.7 %all-gather.11.cloned.1.call-start = ((), (), s32[]{:S(2)}) async-start(), calls=%async_computation.4 | async-start | bytes 7077888 | tf_op jit(solution)/shard_map/all_gather | solution.py:72
  414.3 200.0 %reduce-scatter.2.cloned.1.call-start = ((), (), s32[]{:S(2)}) async-start(), calls=%async_computation.5 | async-start | bytes 10027008 | tf_op jit(solution)/shard_map/reduce_scatter | solution.py:76
Sparse Core Ops, SparseCore 0:
  9.8 50.2 all-gather.4
  62.0 44.6 all-gather.6
  413.9 64.5 all-gather.8
  480.1 20.2 all-gather.10
  502.8 111.4 reduce-scatter.1
where the time goes:
time: 627 us; the launch traced here: 623 us
  waiting for transfers between devices  278 us (44%)
  matrix products  115 us (18%)
  local copies, waits for them, and re-layouts  110 us (18%)
  other arithmetic  75.8 us (12%)
  loops' own time  29.9 us (5%)
  between operations  13.8 us (2%)
    reduce_scatter x1, waiting for transfers between devices, body(): lax.psum_scatter(lax.dot_general(head_columns, cotangent, (((0,), (0,)),...  106 us
    dynamic_slice x64, local copies, waits for them, and re-layouts, body(): lax.scan(one_block, start_state, (key_stack, value_stack, block_columns))  96.5 us
    all_gather x1, waiting for transfers between devices, body(): all_heads = lax.all_gather(attended, 'row', axis=1, tiled=True)  64.1 us
    dot_general x16, matrix products, attend_block(): jnp.einsum('thu,uhd->thd', weights.astype(jnp.bfloat16), value_heads, pre...  58.4 us
    all_gather x1, waiting for transfers between devices, body(): key_piece = lax.all_gather(keys, ('col', 'ctx'), axis=0, tiled=True)  48.1 us
    all_gather x1, waiting for transfers between devices, body(): value_piece = lax.all_gather(values, ('col', 'ctx'), axis=0, tiled=True)  46.5 us
    dot_general x16, matrix products, attend_block(): jnp.einsum('thd,uhd->thu', query_heads, key_heads, preferred_element_type...  38.2 us
    another operation x1, loops' own time, body(): lax.scan(one_block, start_state, (key_stack, value_stack, block_columns))  29.9 us
  transfers between devices with their start and end apart: 5, of which 5 were waited for; matrix products, arithmetic and copies ran while one was open for 3% of the time, Pallas kernels for 0%

commit v1 on v0

--- a/solution.py
+++ b/solution.py
@@ -47,7 +47,11 @@
         jnp.zeros((tok_rows, head_count, HD), jnp.float32),
     )
     key_piece = lax.all_gather(keys, ("col", "ctx"), axis=0, tiled=True)
-    value_piece = lax.all_gather(values, ("col", "ctx"), axis=0, tiled=True)
+    devices = lax.axis_size(("col", "ctx"))
+    repeats = [devices if d == 0 else 1 for d in range(values.ndim)]
+    value_piece = lax.all_to_all(
+        jnp.tile(values, repeats), ("col", "ctx"), split_axis=0, concat_axis=0, tiled=True
+    )
     block_count = key_piece.shape[0] // BLOCK
     key_stack = key_piece.reshape(block_count, BLOCK, feature_width)
     value_stack = value_piece.reshape(block_count, BLOCK, feature_width)

time: 627 us -> 624 us (level)
  waiting for transfers between devices: 278 us -> 349 us
  matrix products: 115 us -> 80.3 us
  other arithmetic: 75.8 us -> 46 us
  local copies, waits for them, and re-layouts: 110 us -> 91 us
  starting transfers between devices: 0.19 us -> 10.3 us
    all_to_all x0 -> x1, waiting for transfers between devices: none -> 164 us  [body(): lax.all_to_all(jnp.tile(values, repeats), ('col', 'ctx'), split_axis=0, c...]
    all_gather x1, waiting for transfers between devices: 48.1 us -> 0.01 us  [body(): key_piece = lax.all_gather(keys, ('col', 'ctx'), axis=0, tiled=True)]
    all_gather x1 -> x0, waiting for transfers between devices: 46.5 us -> none  [body(): value_piece = lax.all_gather(values, ('col', 'ctx'), axis=0, tiled=True)]
    dot_general x16, matrix products: 58.4 us -> 24.7 us  [attend_block(): jnp.einsum('thu,uhd->thd', weights.astype(jnp.bfloat16), value_heads, pre...]
    dynamic_slice x64, local copies, waits for them, and re-layouts: 96.5 us -> 69.1 us  [body(): lax.scan(one_block, start_state, (key_stack, value_stack, block_columns))]
    add x16, other arithmetic: 20.6 us -> 0.33 us  [attend_block(): new_sum = run_sum * correction + jnp.sum(weights, axis=2)]
    max x16, other arithmetic: 10.6 us -> 0.11 us  [attend_block(): new_max = jnp.maximum(run_max, jnp.max(scores, axis=2))]
    all_to_all x0 -> x1, starting transfers between devices: none -> 10.1 us  [body(): lax.all_to_all(jnp.tile(values, repeats), ('col', 'ctx'), split_axis=0, c...]
  transfers between devices with their start and end apart: 5 -> 5, of which waited for: 5 -> 4; matrix products, arithmetic and copies ran while one was open for 3% -> 3% of each run, Pallas kernels for 0% -> 0%
where the time goes in v1:
time: 624 us; the launch traced here: 621 us
  waiting for transfers between devices  349 us (56%)
  local copies, waits for them, and re-layouts  91 us (15%)
  matrix products  80.3 us (13%)
  other arithmetic  46 us (7%)
  loops' own time  30.6 us (5%)
  between operations  13.8 us (2%)
  starting transfers between devices  10.3 us (2%)
    all_to_all x1, waiting for transfers between devices, body(): lax.all_to_all(jnp.tile(values, repeats), ('col', 'ctx'), split_axis=0, c...  164 us
    reduce_scatter x1, waiting for transfers between devices, body(): lax.psum_scatter(lax.dot_general(head_columns, cotangent, (((0,), (0,)),...  106 us
    dynamic_slice x64, local copies, waits for them, and re-layouts, body(): lax.scan(one_block, start_state, (key_stack, value_stack, block_columns))  69.1 us
    all_gather x1, waiting for transfers between devices, body(): all_heads = lax.all_gather(attended, 'row', axis=1, tiled=True)  66.3 us
    dot_general x16, matrix products, attend_block(): jnp.einsum('thd,uhd->thu', query_heads, key_heads, preferred_element_type...  37.4 us
    another operation x1, loops' own time, body(): lax.scan(one_block, start_state, (key_stack, value_stack, block_columns))  30.6 us
    dot_general x16, matrix products, attend_block(): jnp.einsum('thu,uhd->thd', weights.astype(jnp.bfloat16), value_heads, pre...  24.7 us
    reduce_sum x16, other arithmetic, attend_block(): new_sum = run_sum * correction + jnp.sum(weights, axis=2)  21.9 us
  transfers between devices with their start and end apart: 5, of which 4 were waited for; matrix products, arithmetic and copies ran while one was open for 3% of the time, Pallas kernels for 0%

profile of v1, /device:TPU:1, one launch (start us, length us, event | category | flops | bytes accessed | tf_op | source)
XLA Modules:
  0.0 621.0 jit_solution(18026039779905775649)
XLA Ops:
  8.4 3.2 tile.2
  11.6 10.1 %all-to-all-start = ((bf16[16,512,384]{1,2,0:T(8,128)(2,1)}), bf16[16,512,384]{1,2,0:T(8,128)(2,1)}, u32[]{:S(2)}, u32[]{:S(2)}) async-start(bf16[16,512,384]{1,2,0:T(8,128)(2,1)} %tile.2), calls=%async_computation | async-start | bytes 12582912 | tf_op jit(solution)/shard_map/all_to_all | solution.py:52
  24.9 163.6 %all-to-all-done = bf16[16,512,384]{1,2,0:T(8,128)(2,1)} async-done(((bf16[16,512,384]{1,2,0:T(8,128)(2,1)}), bf16[16,512,384]{1,2,0:T(8,128)(2,1)}, u32[]{:S(2)}, u32[]{:S(2)}) %all-to-all-start) | async-done | bytes 6291488 | tf_op jit(solution)/shard_map/all_to_all | solution.py:52
  189.1 218.5 %while.22 = (s32[]{:T(128)}, f32[512,3]{0,1:T(4,128)S(1)}, f32[512,3]{0,1:T(4,128)}, f32[512,3,128]{0,2,1:T(8,128)}, s32[16]{0:T(128)}, /*index=5*/s32[1,16]{1,0...) while((s32[]{:T(128)}, f32[512,3]{0,1:T(4,128)S(1)}, ...), condition=%wide.region_3.4_spmd.clone, body=%wide.region_0.3_spmd.clone.sunk | while | flops 413474304 | bytes 20988212 | solution.py:67
  195.4 2.3 bitcast_reduce_fusion.2
  209.1 2.3 bitcast_reduce_fusion.2
  222.8 2.3 bitcast_reduce_fusion.2
  236.4 2.3 bitcast_reduce_fusion.2
  250.1 2.3 bitcast_reduce_fusion.2
  263.7 2.3 bitcast_reduce_fusion.2
  277.4 2.3 bitcast_reduce_fusion.2
  291.1 2.3 bitcast_reduce_fusion.2
  304.7 2.3 bitcast_reduce_fusion.2
  318.4 2.3 bitcast_reduce_fusion.2
  332.0 2.3 bitcast_reduce_fusion.2
  345.7 2.3 bitcast_reduce_fusion.2
  359.3 2.3 bitcast_reduce_fusion.2
  373.0 2.3 bitcast_reduce_fusion.2
  386.7 2.3 bitcast_reduce_fusion.2
  410.4 66.3 %all-gather.6.cloned.1.call-done = bf16[512,6144]{0,1:T(8,128)(2,1)} async-done(((bf16[512,384]{0,1:T(8,128)(2,1)}), bf16[512,6144]{0,1:T(8,128)(2,1)}) %all-gather.6.cloned.1.call-update) | async-done | bytes 6291472 | tf_op jit(solution)/shard_map/all_gather | solution.py:72
  476.7 9.9 %fusion.19 = f32[6144,384]{1,0:T(8,128)} fusion(bf16[512,6144]{0,1:T(8,128)(2,1)} %all-gather.6.cloned.1.call-done, bf16[512,384]{1,0:T(8,128)(2,1)S(1)} %copy-done), kind=kOutput, calls=%fused_computation.27 | convolution fusion | flops 2415919104 | bytes 16121856 | tf_op jit(solution)/shard_map/dot_general | solution.py:81
  486.6 12.2 %all-gather.8.cloned.1.call-done = bf16[6144,384]{1,0:T(8,128)(2,1)} async-done(((bf16[3072,384]{1,0:T(8,128)(2,1)}), bf16[6144,384]{1,0:T(8,128)(2,1)}) %all-gather.8.cloned.1.call-update) | async-done | bytes 4718608 | tf_op jit(solution)/shard_map/all_gather | solution.py:76
  498.8 8.3 %convolution_convert_fusion = bf16[512,384]{1,0:T(8,128)(2,1)} fusion(bf16[512,6144]{0,1:T(8,128)(2,1)} %all-gather.6.cloned.1.call-done, bf16[6144,384]{1,0:T(8,128)(2,1)} %all-gather.8.cloned.1.call-done), kind=kOutput, calls=%fused_computation.23 | convolution fusion | flops 2416115712 | bytes 11403264 | tf_op jit(solution)/shard_map/dot_general | solution.py:74
  507.1 105.5 %reduce-scatter.2.cloned.1.call-done = f32[384,384]{1,0:T(8,128)} async-done(((f32[6144,384]{1,0:T(8,128)}), f32[384,384]{1,0:T(8,128)}) %reduce-scatter.2.cloned.1.call-update) | async-done | bytes 589840 | tf_op jit(solution)/shard_map/reduce_scatter | solution.py:80
  (312 shorter events, 162.4 us)
Async XLA Ops:
  7.2 469.6 %copy-start = (bf16[512,384]{1,0:T(8,128)(2,1)S(1)}, bf16[512,384]{1,0:T(8,128)(2,1)}, u32[]{:S(2)}) copy-start(bf16[512,384]{1,0:T(8,128)(2,1)} %param.16) | copy-start | bytes 1179652
  11.6 10.9 %copy-start.3 = (bf16[512,384]{1,0:T(8,128)(2,1)S(1)}, bf16[512,384]{1,0:T(8,128)(2,1)}, u32[]{:S(2)}) copy-start(bf16[512,384]{1,0:T(8,128)(2,1)} %param.12) | copy-start | bytes 1179652
  11.6 176.9 %all-to-all-start = ((bf16[16,512,384]{1,2,0:T(8,128)(2,1)}), bf16[16,512,384]{1,2,0:T(8,128)(2,1)}, u32[]{:S(2)}, u32[]{:S(2)}) async-start(bf16[16,512,384]{1,2,0:T(8,128)(2,1)} %tile.2), calls=%async_computation | async-start | bytes 12582912 | tf_op jit(solution)/shard_map/all_to_all | solution.py:52
  21.7 166.8 %all-gather.4.cloned.1.call-start = ((), (), s32[]{:S(2)}) async-start(), calls=%async_computation.2 | async-start | bytes 6684672 | tf_op jit(solution)/shard_map/all_gather | solution.py:49
  22.5 454.3 %all-gather.6.cloned.1.call-start = ((), (), s32[]{:S(2)}) async-start(), calls=%async_computation.3 | async-start | bytes 6684672 | tf_op jit(solution)/shard_map/all_gather | solution.py:72
  199.2 2.6 copy-start.5
  212.9 2.6 copy-start.5
  226.5 2.6 copy-start.5
  240.2 2.6 copy-start.5
  253.9 2.6 copy-start.5
  267.5 2.6 copy-start.5
  281.2 2.6 copy-start.5
  293.4 2.5 copy-start.1
  294.8 2.6 copy-start.5
  308.5 2.6 copy-start.5
  322.2 2.6 copy-start.5
  335.8 2.6 copy-start.5
  349.5 2.6 copy-start.5
  363.1 2.6 copy-start.5
  376.8 2.6 copy-start.5
  390.5 2.6 copy-start.5
  404.1 2.6 copy-start.5
  409.6 89.2 %all-gather.8.cloned.1.call-start = ((), (), s32[]{:S(2)}) async-start(), calls=%async_computation.4 | async-start | bytes 7077888 | tf_op jit(solution)/shard_map/all_gather | solution.py:76
  410.4 202.3 %reduce-scatter.2.cloned.1.call-start = ((), (), s32[]{:S(2)}) async-start(), calls=%async_computation.5 | async-start | bytes 10027008 | tf_op jit(solution)/shard_map/reduce_scatter | solution.py:80
  (47 other events, 74.1 us)
Sparse Core Ops, SparseCore 0:
  24.4 152.5 all-gather.3
  409.7 66.9 all-gather.5
  478.5 20.2 all-gather.7
  501.2 111.4 reduce-scatter.1
